TPU v7x, 128 devices: a whole 4x4x4 slice. The times are simulated.
128 devices in a mesh: gx: 8 (over z_hi, x), gy: 16 (over z_lo, y, core).
Axes of the slice: x: 4, y: 4, z: 4 (z_hi: 2, z_lo: 2; z = z_hi * 2 + z_lo), core: 2. Of those that a mesh axis runs over, the one named last changes fastest.
Arguments:
- coarse: bfloat16 [12, 128, 512], P(None, ('gx', 'gy')), may hold values from -6 to 6
- weight_one: bfloat16 [3, 3, 12, 64], replicated, may hold values from -0.625 to 0.625
- weight_two: bfloat16 [3, 3, 64, 64], replicated, may hold values from -0.25 to 0.25
- weight_three: bfloat16 [3, 3, 64, 256], replicated, may hold values from -0.25 to 0.25
- weight_four: bfloat16 [3, 3, 64, 256], replicated, may hold values from -0.25 to 0.25
- weight_five: bfloat16 [3, 3, 64, 12], replicated, may hold values from -0.25 to 0.25
- bias_one: float32 [64], replicated, may hold values from -3 to 3
- bias_two: float32 [64], replicated, may hold values from -3 to 3
- bias_three: float32 [256], replicated, may hold values from -3 to 3
- bias_four: float32 [256], replicated, may hold values from -3 to 3
- bias_five: float32 [12], replicated, may hold values from -3 to 3
- cotangent: bfloat16 [12, 512, 2048], P(None, 'gx', 'gy'), may hold values from -6 to 6
Outputs:
- fine: float32 [12, 512, 2048], P(None, 'gx', 'gy')
- grad_w1: float32 [3, 3, 12, 64], replicated
- grad_w2: float32 [3, 3, 64, 64], replicated
- grad_w3: float32 [3, 3, 64, 256], replicated
- grad_w4: float32 [3, 3, 64, 256], replicated
- grad_w5: float32 [3, 3, 64, 12], replicated
- grad_b1: float32 [64], replicated
- grad_b2: float32 [64], replicated
- grad_b3: float32 [256], replicated
- grad_b4: float32 [256], replicated
- grad_b5: float32 [12], replicated
All inputs are finite; a program needn't handle non-finite values.
Results may differ from a plain program's by a relative error of at most 0.013.
Values may be sent and summed in bfloat16 or wider, within the bound.
A program may use at most 128 MiB of HBM per device.

v0:
```python
import jax
import jax.numpy as jnp
from jax import lax
from jax.sharding import PartitionSpec as P


def padded_2(block, sides, width):
    for axis, dim in sides:
        count = lax.axis_size(axis)
        forward = [(i, i + 1) for i in range(count - 1)]
        backward = [(target, source) for source, target in forward]
        low = lax.ppermute(
            lax.slice_in_dim(block, block.shape[dim] - width, None, axis=dim), axis, forward
        )
        high = lax.ppermute(lax.slice_in_dim(block, 0, width, axis=dim), axis, backward)
        block = jnp.concatenate([low, block, high], axis=dim)
    return block


def conv_valid(padded, weight, bias):
    rows = padded.shape[1] - 2
    cols = padded.shape[2] - 2
    total = jnp.zeros((weight.shape[3], rows, cols), jnp.float32) + bias[:, None, None]
    for row_off in range(3):
        for col_off in range(3):
            total = total + jnp.einsum(
                "chw,co->ohw",
                padded[:, row_off : row_off + rows, col_off : col_off + cols],
                weight[row_off, col_off],
                preferred_element_type=jnp.float32,
            )
    return total


def conv_back(padded, weight):
    rows = padded.shape[1] - 2
    cols = padded.shape[2] - 2
    total = jnp.zeros((weight.shape[2], rows, cols), jnp.float32)
    for row_off in range(3):
        for col_off in range(3):
            total = total + jnp.einsum(
                "ohw,co->chw",
                padded[:, 2 - row_off : 2 - row_off + rows, 2 - col_off : 2 - col_off + cols],
                weight[row_off, col_off],
                preferred_element_type=jnp.float32,
            )
    return total


def weight_grad(padded, grad):
    rows = grad.shape[1]
    cols = grad.shape[2]
    pieces = []
    for row_off in range(3):
        for col_off in range(3):
            pieces.append(
                jnp.einsum(
                    "chw,ohw->co",
                    padded[:, row_off : row_off + rows, col_off : col_off + cols],
                    grad,
                    preferred_element_type=jnp.float32,
                )
            )
    stacked = jnp.stack(pieces)
    return stacked.reshape(3, 3, stacked.shape[1], stacked.shape[2])


def squash(value):
    return jnp.tanh(value)


def slopes(act):
    act_f = act.astype(jnp.float32)
    return 1.0 - act_f * act_f


def shuffle(value):
    chans, rows, cols = value.shape
    return (
        value.reshape(chans // 4, 2, 2, rows, cols)
        .transpose(0, 3, 1, 4, 2)
        .reshape(chans // 4, 2 * rows, 2 * cols)
    )


def unshuffle(value):
    chans, rows, cols = value.shape
    return (
        value.reshape(chans, rows // 2, 2, cols // 2, 2)
        .transpose(0, 2, 4, 1, 3)
        .reshape(4 * chans, rows // 2, cols // 2)
    )


def inside(halo, rows, cols, grain):
    row = lax.axis_index("gx") * rows * grain - halo + jnp.arange(rows * grain + 2 * halo)
    col = lax.axis_index("gy") * cols * grain - halo + jnp.arange(cols * grain + 2 * halo)
    row_ok = (row >= 0) & (row < rows * grain * lax.axis_size("gx"))
    col_ok = (col >= 0) & (col < cols * grain * lax.axis_size("gy"))
    return (row_ok[:, None] & col_ok[None, :])[None]


def trim(value, width):
    return value[:, width : value.shape[1] - width, width : value.shape[2] - width]


def local_terms(padded, grad):
    return (weight_grad(padded, grad), jnp.sum(grad.astype(jnp.float32), axis=(1, 2)))


def local(
    coarse,
    weight_one,
    weight_two,
    weight_three,
    weight_four,
    weight_five,
    bias_one,
    bias_two,
    bias_three,
    bias_four,
    bias_five,
    cotangent,
):
    tile = lax.all_to_all(coarse, "gy", split_axis=2, concat_axis=1, tiled=True)
    rows = tile.shape[1]
    cols = tile.shape[2]
    sides = (("gx", 1), ("gy", 2))
    zero = jnp.bfloat16(0)
    pad_zero = padded_2(tile, sides, 6)
    pad_cot = padded_2(cotangent, sides, 11)

    def clip(value, halo, grain):
        return jnp.where(inside(halo, rows, cols, grain), value.astype(jnp.bfloat16), zero)

    act_one = clip(squash(conv_valid(pad_zero, weight_one, bias_one)), 5, 1)
    act_two = clip(squash(conv_valid(act_one, weight_two, bias_two)), 4, 1)
    act_three = clip(shuffle(squash(conv_valid(act_two, weight_three, bias_three))), 6, 2)
    act_four = clip(shuffle(squash(conv_valid(act_three, weight_four, bias_four))), 10, 4)
    pad_four = trim(act_four, 9)
    fine = conv_valid(pad_four, weight_five, bias_five)
    layer_five = local_terms(pad_four, cotangent)
    back_four = unshuffle(clip(conv_back(pad_cot, weight_five) * slopes(act_four), 10, 4))
    layer_four = local_terms(trim(act_three, 5), trim(back_four, 5))
    back_three = unshuffle(
        clip(conv_back(back_four, weight_four) * slopes(trim(act_three, 2)), 4, 2)
    )
    layer_three = local_terms(trim(act_two, 3), trim(back_three, 2))
    back_two = clip(conv_back(back_three, weight_three) * slopes(trim(act_two, 3)), 1, 1)
    layer_two = local_terms(trim(act_one, 4), trim(back_two, 1))
    back_one = (conv_back(back_two, weight_two) * slopes(trim(act_one, 5))).astype(jnp.bfloat16)
    layer_one = local_terms(trim(pad_zero, 5), back_one)
    totals = lax.psum(
        (
            layer_one[0],
            layer_two[0],
            layer_three[0],
            layer_four[0],
            layer_five[0],
            layer_one[1],
            layer_two[1],
            layer_three[1],
            layer_four[1],
            layer_five[1],
        ),
        ("gx", "gy"),
    )
    cells = 16 * rows * lax.axis_size("gx") * cols * lax.axis_size("gy")
    scale = jnp.float32(cells) ** (-0.5)
    return (fine,) + tuple((scale * total for total in totals))


def solution(mesh):
    in_specs = (
        P(None, ("gx", "gy"), None),
        P(),
        P(),
        P(),
        P(),
        P(),
        P(),
        P(),
        P(),
        P(),
        P(),
        P(None, "gx", "gy"),
    )
    out_specs = (P(None, "gx", "gy"), P(), P(), P(), P(), P(), P(), P(), P(), P(), P())
    return jax.shard_map(local, mesh=mesh, in_specs=in_specs, out_specs=out_specs, check_vma=False)
```

profile of v0, /device:TPU:1, one launch (start us, length us, event | category | flops | bytes accessed | tf_op | source)
XLA Modules:
  0.0 527.5 jit_solution(14935861701973462244)
XLA Ops:
  10.9 7.3 %all-to-all-start = ((bf16[16,2,192]{2,1,0:T(2,128)(2,1)}), bf16[16,2,192]{2,1,0:T(2,128)(2,1)S(1)}, u32[]{:S(2)}, u32[]{:S(2)}) async-start(bf16[16,2,192]{2,1,0:T(2,128)(2,1)} %reshape.410), calls=%async_computation | async-start | bytes 32768 | tf_op jit(solution)/shard_map/all_to_all | solution.py:125
  22.9 4.8 collective-permute-start.4
  28.9 2.3 collective-permute-start
  32.6 5.9 %collective-permute-done = bf16[12,6,32]{2,0,1:T(8,128)(2,1)S(1)} collective-permute-done((bf16[12,6,32]{2,0,1:T(8,128)(2,1)S(1)}, bf16[12,6,32]{2,0,1:T(8,128)(2,1)S(1)}, u32[]{:S(2)}, u32[]{:S(2)}) %collective-permute-start) | collective-permute-done | bytes 4640 | tf_op jit(solution)/shard_map/ppermute | solution.py:12
  38.7 4.3 collective-permute-start.2
  46.9 2.3 collective-permute-done.3
  59.9 4.6 copy.173
  69.9 2.8 fusion.234
  72.7 2.8 fusion.236
  75.5 2.5 fusion.238
  78.0 6.1 %fusion.56 = bf16[256,42,74]{0,2,1:T(8,128)(2,1)} fusion(f32[42,74,256]{2,1,0:T(8,128)S(1)} %fusion.224, f32[42,74,256]{2,1,0:T(8,128)S(1)} %fusion.226, f32[42,74,256]{2,1,0:T(8,128)S(1)} %fusion.228, f32[42,74,256]{2,1,0:T(8,128)S(1)} %fusion.230, f32[42,74,256]{2,1,0:T(8,128)S(1)} %fusion.232, f32[42,74,256]{2,1,0:T(8,128)} %fusion.234, ...), kind=kOutput, calls=%fused_computation.60 | convolution fusion | flops 109799424 | bytes 29064192 | tf_op jit(solution)/shard_map/chw,co->ohw/dot_general | solution.py:26
  84.1 3.0 copy.175
  87.1 9.5 %copy.176 = bf16[64,42,2,74,2]{0,4,3,2,1:T(2,128)(2,1)} copy(bf16[64,42,2,74,2]{3,4,2,0,1:T(2,128)(2,1)S(1)} %bitcast.649) | data formatting | bytes 3182592 | tf_op jit(solution)/shard_map/convert_element_type | solution.py:134
  96.6 5.6 %convert_element_type.78 = bf16[64,84,148]{0,2,1:T(8,128)(2,1)} reshape(bf16[64,42,2,74,2]{0,4,3,2,1:T(2,128)(2,1)} %copy.176) | data formatting | bytes 3182592 | tf_op jit(solution)/shard_map/convert_element_type | solution.py:134
  102.1 5.1 copy.177
  131.0 2.7 copy.253
  133.8 2.5 copy.251
  136.3 2.5 copy.249
  138.8 2.5 copy.247
  141.3 2.5 copy.245
  143.8 2.5 copy.243
  146.4 2.5 copy.241
  148.9 2.5 copy.237
  151.4 2.5 copy.239
  153.9 2.7 add_bitcast_fusion
  160.5 2.4 collective-permute-start.7
  167.6 3.0 fusion.244
  170.7 3.1 fusion.246
  173.7 3.1 fusion.248
  176.8 3.0 fusion.250
  179.8 3.0 fusion.252
  182.8 3.0 fusion.254
  185.9 3.1 fusion.256
  189.0 3.0 fusion.258
  192.0 14.3 %fusion.19 = bf16[64,84,148]{1,0,2:T(8,128)(2,1)S(1)} fusion(f32[84,148,64]{0,2,1:T(8,128)} %fusion.244, f32[84,148,64]{0,2,1:T(8,128)} %fusion.246, f32[84,148,64]{0,2,1:T(8,128)} %fusion.248, f32[84,148,64]{0,2,1:T(8,128)} %fusion.250, f32[84,148,64]{0,2,1:T(8,128)} %fusion.252, f32[84,148,64]{0,2,1:T(8,128)} %fusion.254, f32[84,148,64]{0,2,1:T(8,128)} %fusion.258, ...), kind=kOutput, calls=%fused_computation.21 | convolution fusion | flops 31030272 | bytes 30106624 | tf_op jit(solution)/shard_map/ohw,co->chw/dot_general | solution.py:41
  206.3 3.8 copy.190
  210.1 5.7 %reshape.311 = bf16[64,42,2,74,2]{0,4,3,2,1:T(2,128)(2,1)} reshape(bf16[64,84,148]{0,2,1:T(8,128)(2,1)} %copy.190) | data formatting | bytes 3182592 | tf_op jit(solution)/shard_map/reshape | solution.py:89
  215.8 11.8 %copy.191 = bf16[64,2,2,42,74]{4,2,1,0,3:T(2,128)(2,1)S(1)} copy(bf16[64,2,2,42,74]{0,2,4,1,3:T(2,128)(2,1)} %bitcast.648) | data formatting | bytes 3182592 | tf_op jit(solution)/shard_map/transpose | solution.py:90
  233.2 2.0 slice.916
  237.9 2.2 fusion.157
  240.1 2.2 copy.201
  242.4 5.0 copy.202
  247.4 2.2 fusion.117
  249.6 2.1 convolution_add_fusion.26
  276.4 2.0 copy.300
  290.1 77.8 %all-reduce = (f32[3,3,12,64]{3,2,1,0:T(8,128)S(1)}, f32[3,3,64,12]{2,3,1,0:T(8,128)S(1)}, f32[64]{0:T(128)S(1)}, f32[64]{0:T(128)S(1)}, f32[256]{0:T(256)S(1)}, /*index=5*/f32[256]{0:T(256)S(1)}, f32[12]{0:T(128)S(1)}) all-reduce(f32[3,3,12,64]{3,2,1,0:T(8,128)S(1)} %bitcast.656, ...), channel_id=1, replica_groups=mesh['gx'=8,'gy'=16] {'gx','gy'}, use_global_device_ids=true, to_apply=%region_0.1 | all-reduce | flops 14476 | bytes 115808 | tf_op jit(solution)/shard_map/psum | solution.py:153
  370.8 145.5 %all-reduce.4.cloned.1.call-done = (f32[3,3,64,64]{3,2,1,0:T(8,128)}, f32[3,3,64,256]{3,2,1,0:T(8,128)}, f32[3,3,64,256]{3,2,1,0:T(8,128)}) async-done(((f32[3,3,64,64]{3,2,1,0:T(8,128)}, f32[3,3,64,256]{3,2,1,0:T(8,128)}, f32[3,3,64,256]{3,2,1,0:T(8,128)}), (f32[3,3,64,64]{3,2,1,0:T(8,128)}, f32[3,3,64,256]{3,2,1,0:T(8,128)}, f32[3,3,64,256]{3,2,1,0:T(8,128)})) %all-reduce.4.cloned.1.call-update) | async-done | bytes 1327120 | tf_op jit(solution)/shard_map/psum | solution.py:153
  518.0 2.4 broadcast_multiply_fusion
  (273 shorter events, 111.9 us)
Async XLA Ops:
  7.2 37.9 %copy-start.19 = (bf16[12,64,128]{2,1,0:T(8,128)(2,1)S(1)}, bf16[12,64,128]{2,1,0:T(8,128)(2,1)}, u32[]{:S(2)}) copy-start(bf16[12,64,128]{2,1,0:T(8,128)(2,1)} %param.23) | copy-start | bytes 589828
  8.7 40.7 %copy-start.36 = (bf16[3,3,12,64]{3,2,1,0:T(8,128)(2,1)S(1)}, bf16[3,3,12,64]{3,2,1,0:T(8,128)(2,1)}, u32[]{:S(2)}) copy-start(bf16[3,3,12,64]{3,2,1,0:T(8,128)(2,1)} %param.13) | copy-start | bytes 41476
  10.9 17.4 %all-to-all-start = ((bf16[16,2,192]{2,1,0:T(2,128)(2,1)}), bf16[16,2,192]{2,1,0:T(2,128)(2,1)S(1)}, u32[]{:S(2)}, u32[]{:S(2)}) async-start(bf16[16,2,192]{2,1,0:T(2,128)(2,1)} %reshape.410), calls=%async_computation | async-start | bytes 32768 | tf_op jit(solution)/shard_map/all_to_all | solution.py:125
  18.2 498.1 %all-reduce.4.cloned.1.call-start = ((), (), s32[]{:S(2)}) async-start(), calls=%async_computation.1 | async-start | bytes 2949120 | tf_op jit(solution)/shard_map/psum | solution.py:153
  20.4 137.2 %collective-permute-start.5 = (bf16[12,11,128]{1,0,2:T(8,128)(2,1)}, bf16[12,11,128]{1,0,2:T(8,128)(2,1)}, u32[]{:S(2)}, u32[]{:S(2)}) collective-permute-start(bf16[12,11,128]{1,0,2:T(8,128)(2,1)} %copy.188), channel_id=1, source_target_pairs={{16,0},{32,16},{48,32},{64,48},{80,64},{96,80},{112,96},{17,1},{33... | collective-permute-start | bytes 101384 | tf_op jit(solution)/shard_map/ppermute | solution.py:15
  22.9 134.7 %collective-permute-start.4 = (bf16[12,11,128]{1,0,2:T(8,128)(2,1)}, bf16[12,11,128]{1,0,2:T(8,128)(2,1)}, u32[]{:S(2)}, u32[]{:S(2)}) collective-permute-start(bf16[12,11,128]{1,0,2:T(8,128)(2,1)} %copy.187), channel_id=1, source_target_pairs={{0,16},{16,32},{32,48},{48,64},{64,80},{80,96},{96,112},{1,17},{17... | collective-permute-start | bytes 101384 | tf_op jit(solution)/shard_map/ppermute | solution.py:12
  28.9 22.1 %copy-start.31 = (bf16[12,16,32]{2,0,1:T(8,128)(2,1)}, bf16[12,16,32]{2,0,1:T(8,128)(2,1)S(1)}, u32[]{:S(2)}) copy-start(bf16[12,16,32]{2,0,1:T(8,128)(2,1)S(1)} %copy.169) | copy-start | bytes 36868
  28.9 9.6 %collective-permute-start = (bf16[12,6,32]{2,0,1:T(8,128)(2,1)S(1)}, bf16[12,6,32]{2,0,1:T(8,128)(2,1)S(1)}, u32[]{:S(2)}, u32[]{:S(2)}) collective-permute-start(bf16[12,6,32]{2,0,1:T(8,128)(2,1)S(1)} %get-tuple-element.72), channel_id=1, source_target_pairs={{0,16},{16,32},{32,48},{48,64},{64,80},{80,96},{96,112},{1,17},{17... | collective-permute-start | bytes 13832 | tf_op jit(solution)/shard_map/ppermute | solution.py:12
  31.3 7.3 %collective-permute-start.1 = (bf16[12,6,32]{2,0,1:T(8,128)(2,1)S(1)}, bf16[12,6,32]{2,0,1:T(8,128)(2,1)S(1)}, u32[]{:S(2)}, u32[]{:S(2)}) collective-permute-start(bf16[12,6,32]{2,0,1:T(8,128)(2,1)S(1)} %get-tuple-element.71), channel_id=1, source_target_pairs={{16,0},{32,16},{48,32},{64,48},{80,64},{96,80},{112,96},{17,1},{33... | collective-permute-start | bytes 13832 | tf_op jit(solution)/shard_map/ppermute | solution.py:15
  38.6 4.5 copy-start.39
  38.6 4.5 copy-start.37
  38.6 12.8 %copy-start.8 = (bf16[12,28,32]{2,0,1:T(8,128)(2,1)}, bf16[12,28,32]{2,0,1:T(8,128)(2,1)S(1)}, u32[]{:S(2)}) copy-start(bf16[12,28,32]{2,0,1:T(8,128)(2,1)S(1)} %constant_dynamic-update-slice_fusion) | copy-start | bytes 64516
  38.7 8.2 %collective-permute-start.2 = (bf16[12,28,6]{2,0,1:T(8,128)(2,1)S(1)}, bf16[12,28,6]{2,0,1:T(8,128)(2,1)S(1)}, u32[]{:S(2)}, u32[]{:S(2)}) collective-permute-start(bf16[12,28,6]{2,0,1:T(8,128)(2,1)S(1)} %get-tuple-element.69), channel_id=1, source_target_pairs={{0,1},{1,2},{2,3},{3,4},{4,5},{5,6},{6,7},{7,8},{8,9},{9,10},{10,1... | collective-permute-start | bytes 12104 | tf_op jit(solution)/shard_map/ppermute | solution.py:12
  43.1 6.1 %collective-permute-start.3 = (bf16[12,28,6]{2,0,1:T(8,128)(2,1)S(1)}, bf16[12,28,6]{2,0,1:T(8,128)(2,1)S(1)}, u32[]{:S(2)}, u32[]{:S(2)}) collective-permute-start(bf16[12,28,6]{2,0,1:T(8,128)(2,1)S(1)} %get-tuple-element.70), channel_id=1, source_target_pairs={{1,0},{2,1},{3,2},{4,3},{5,4},{6,5},{7,6},{8,7},{9,8},{10,9},{11,1... | collective-permute-start | bytes 12104 | tf_op jit(solution)/shard_map/ppermute | solution.py:15
  46.9 4.7 copy-start.17
  49.2 2.5 copy-start.15
  50.2 2.3 copy-start.44
  53.5 2.2 copy-start.6
  56.0 2.2 copy-start.3
  75.5 2.5 copy-start.42
  107.2 1.9 copy-start.33
  121.1 3.4 copy-start.12
  146.3 7.6 %copy-start.46 = (f32[12]{0:T(128)S(1)}, f32[12]{0:T(128)}, u32[]{:S(2)}) copy-start(f32[12]{0:T(128)} %param.22) | copy-start | bytes 148
  153.9 2.7 copy-start.13
  158.6 6.1 %collective-permute-start.6 = (bf16[12,86,11]{1,0,2:T(8,128)(2,1)S(1)}, bf16[12,86,11]{1,0,2:T(8,128)(2,1)S(1)}, u32[]{:S(2)}, u32[]{:S(2)}) collective-permute-start(bf16[12,86,11]{1,0,2:T(8,128)(2,1)S(1)} %get-tuple-element.65), channel_id=1, source_target_pairs={{0,1},{1,2},{2,3},{3,4},{4,5},{5,6},{6,7},{7,8},{8,9},{9,10},{10,1... | collective-permute-start | bytes 68120 | tf_op jit(solution)/shard_map/ppermute | solution.py:12
  160.5 5.4 %collective-permute-start.7 = (bf16[12,86,11]{1,0,2:T(8,128)(2,1)S(1)}, bf16[12,86,11]{1,0,2:T(8,128)(2,1)S(1)}, u32[]{:S(2)}, u32[]{:S(2)}) collective-permute-start(bf16[12,86,11]{1,0,2:T(8,128)(2,1)S(1)} %get-tuple-element.66), channel_id=1, source_target_pairs={{1,0},{2,1},{3,2},{4,3},{5,4},{6,5},{7,6},{8,7},{9,8},{10,9},{11,1... | collective-permute-start | bytes 68120 | tf_op jit(solution)/shard_map/ppermute | solution.py:15
  163.8 6.9 %copy-start.34 = (f32[9,64,12]{1,2,0:T(8,128)}, f32[9,64,12]{1,2,0:T(8,128)S(1)}, u32[]{:S(2)}) copy-start(f32[9,64,12]{1,2,0:T(8,128)S(1)} %fusion.220) | copy-start | bytes 82948
  189.0 3.0 copy-start.2
  227.6 1.7 copy-start.21
  247.4 4.3 copy-start
  247.4 4.3 copy-start.23
  254.2 1.6 copy-start.4
  256.3 1.7 copy-start.10
  276.4 2.3 copy-start.11
  276.4 2.3 copy-start.24
  276.4 2.3 copy-start.28
  278.9 1.4 copy-start.9
  279.1 1.5 copy-start.32
  279.1 1.5 copy-start.40
  279.1 1.7 copy-start.16
  279.3 2.3 copy-start.29
  282.1 1.5 copy-start.25
  283.6 1.9 copy-start.30
  286.7 1.9 copy-start.14
  287.3 2.3 copy-start.38
  287.9 2.2 copy-start.35
  288.0 2.2 copy-start.41
  288.6 80.4 %copy-start.26 = (f32[9,64,256]{2,1,0:T(8,128)}, f32[9,64,256]{2,1,0:T(8,128)S(1)}, u32[]{:S(2)}) copy-start(f32[9,64,256]{2,1,0:T(8,128)S(1)} %fusion.130) | copy-start | bytes 1769476
  (9 other events, 10.5 us)
Sparse Core Ops, SparseCore 0:
  369.2 147.1 all-reduce.3
where the time goes:
time: 537 us; the launch traced here: 527 us
  waiting for transfers between devices  155 us (29%)
  matrix products  138 us (26%)
  local copies, waits for them, and re-layouts  96.1 us (18%)
  blocking collectives  77.8 us (14%)
  starting transfers between devices  27.7 us (5%)
  other arithmetic  17.7 us (3%)
  between operations  15.4 us (3%)
    psum x1, waiting for transfers between devices, local(): lax.psum((layer_one[0], layer_two[0], layer_three[0], layer_four[0], laye...  145 us
    psum x1, blocking collectives, local(): lax.psum((layer_one[0], layer_two[0], layer_three[0], layer_four[0], laye...  77.8 us
    dot_general x36, matrix products, conv_back(): jnp.einsum('ohw,co->chw', padded[:, 2 - row_off:2 - row_off + rows, 2 - c...  59.3 us
    dot_general x45, matrix products, conv_valid(): jnp.einsum('chw,co->ohw', padded[:, row_off:row_off + rows, col_off:col_o...  42.6 us
    dot_general x45, matrix products, weight_grad(): jnp.einsum('chw,ohw->co', padded[:, row_off:row_off + rows, col_off:col_o...  36 us
    convert_element_type x8, local copies, waits for them, and re-layouts, clip(): value.astype(jnp.bfloat16)  29.8 us
    dot_general x9, local copies, waits for them, and re-layouts, conv_valid(): jnp.einsum('chw,co->ohw', padded[:, row_off:row_off + rows, col_off:col_o...  22.9 us
    transpose x2, local copies, waits for them, and re-layouts, unshuffle(): return value.reshape(chans, rows // 2, 2, cols // 2, 2).transpose(0, 2, 4...  16.8 us
  transfers between devices with their start and end apart: 10, of which 4 were waited for; matrix products, arithmetic and copies ran while one was open for 22% of the time, Pallas kernels for 0%

commit v1 on v0

--- a/solution.py
+++ b/solution.py
@@ -151,19 +151,22 @@
     back_one = (conv_back(back_two, weight_two) * slopes(trim(act_one, 5))).astype(jnp.bfloat16)
     layer_one = local_terms(trim(pad_zero, 5), back_one)
     totals = lax.psum(
-        (
-            layer_one[0],
-            layer_two[0],
-            layer_three[0],
-            layer_four[0],
-            layer_five[0],
-            layer_one[1],
-            layer_two[1],
-            layer_three[1],
-            layer_four[1],
-            layer_five[1],
+        lax.psum(
+            (
+                layer_one[0],
+                layer_two[0],
+                layer_three[0],
+                layer_four[0],
+                layer_five[0],
+                layer_one[1],
+                layer_two[1],
+                layer_three[1],
+                layer_four[1],
+                layer_five[1],
+            ),
+            "gx",
         ),
-        ("gx", "gy"),
+        "gy",
     )
     cells = 16 * rows * lax.axis_size("gx") * cols * lax.axis_size("gy")
     scale = jnp.float32(cells) ** (-0.5)

time: 537 us -> 515 us (0.959)
  the two profiles are of different devices: /device:TPU:1 before, /device:TPU:25 now
where the time goes in v1:
time: 515 us; the launch traced here: 506 us
  matrix products  132 us (26%)
  waiting for transfers between devices  121 us (23%)
  blocking collectives  97.4 us (19%)
  local copies, waits for them, and re-layouts  95.7 us (19%)
  starting transfers between devices  26.9 us (5%)
  other arithmetic  17.7 us (3%)
  between operations  15.5 us (3%)
    psum x1, waiting for transfers between devices, local(): lax.psum((layer_one[0], layer_two[0], layer_three[0], layer_four[0], laye...  80.9 us
    psum x1, blocking collectives, local(): lax.psum(lax.psum((layer_one[0], layer_two[0], layer_three[0], layer_four...  63.3 us
    dot_general x36, matrix products, conv_back(): jnp.einsum('ohw,co->chw', padded[:, 2 - row_off:2 - row_off + rows, 2 - c...  57.9 us
    dot_general x45, matrix products, conv_valid(): jnp.einsum('chw,co->ohw', padded[:, row_off:row_off + rows, col_off:col_o...  42.6 us
    psum x1, blocking collectives, local(): lax.psum((layer_one[0], layer_two[0], layer_three[0], layer_four[0], laye...  34.1 us
    dot_general x45, matrix products, weight_grad(): jnp.einsum('chw,ohw->co', padded[:, row_off:row_off + rows, col_off:col_o...  31.8 us
    convert_element_type x8, local copies, waits for them, and re-layouts, clip(): value.astype(jnp.bfloat16)  29.8 us
    psum x1, waiting for transfers between devices, local(): lax.psum(lax.psum((layer_one[0], layer_two[0], layer_three[0], layer_four...  26.6 us
  transfers between devices with their start and end apart: 11, of which 5 were waited for; matrix products, arithmetic and copies ran while one was open for 25% of the time, Pallas kernels for 0%

profile of v1, /device:TPU:25, one launch (start us, length us, event | category | flops | bytes accessed | tf_op | source)
XLA Modules:
  0.0 506.3 jit_solution(6619405552091767639)
XLA Ops:
  10.9 6.4 %all-to-all-start = ((bf16[16,2,192]{2,1,0:T(2,128)(2,1)}), bf16[16,2,192]{2,1,0:T(2,128)(2,1)S(1)}, u32[]{:S(2)}, u32[]{:S(2)}) async-start(bf16[16,2,192]{2,1,0:T(2,128)(2,1)} %reshape.410), calls=%async_computation | async-start | bytes 32768 | tf_op jit(solution)/shard_map/all_to_all | solution.py:125
  21.9 4.8 collective-permute-start.4
  27.9 2.3 collective-permute-start
  31.6 5.6 %collective-permute-done = bf16[12,6,32]{2,0,1:T(8,128)(2,1)S(1)} collective-permute-done((bf16[12,6,32]{2,0,1:T(8,128)(2,1)S(1)}, bf16[12,6,32]{2,0,1:T(8,128)(2,1)S(1)}, u32[]{:S(2)}, u32[]{:S(2)}) %collective-permute-start) | collective-permute-done | bytes 4640 | tf_op jit(solution)/shard_map/ppermute | solution.py:12
  37.4 4.5 collective-permute-start.2
  45.8 4.4 collective-permute-done.3
  60.8 4.6 copy.173
  70.8 2.8 fusion.234
  73.6 2.8 fusion.236
  76.4 2.5 fusion.238
  78.9 6.1 %fusion.56 = bf16[256,42,74]{0,2,1:T(8,128)(2,1)} fusion(f32[42,74,256]{2,1,0:T(8,128)S(1)} %fusion.224, f32[42,74,256]{2,1,0:T(8,128)S(1)} %fusion.226, f32[42,74,256]{2,1,0:T(8,128)S(1)} %fusion.228, f32[42,74,256]{2,1,0:T(8,128)S(1)} %fusion.230, f32[42,74,256]{2,1,0:T(8,128)S(1)} %fusion.232, f32[42,74,256]{2,1,0:T(8,128)} %fusion.234, ...), kind=kOutput, calls=%fused_computation.60 | convolution fusion | flops 109799424 | bytes 29064192 | tf_op jit(solution)/shard_map/chw,co->ohw/dot_general | solution.py:26
  85.0 3.0 copy.175
  88.1 9.4 %copy.176 = bf16[64,42,2,74,2]{0,4,3,2,1:T(2,128)(2,1)} copy(bf16[64,42,2,74,2]{3,4,2,0,1:T(2,128)(2,1)S(1)} %bitcast.649) | data formatting | bytes 3182592 | tf_op jit(solution)/shard_map/convert_element_type | solution.py:134
  97.4 5.6 %convert_element_type.78 = bf16[64,84,148]{0,2,1:T(8,128)(2,1)} reshape(bf16[64,42,2,74,2]{0,4,3,2,1:T(2,128)(2,1)} %copy.176) | data formatting | bytes 3182592 | tf_op jit(solution)/shard_map/convert_element_type | solution.py:134
  103.0 5.1 %copy.177 = bf16[64,84,148]{1,0,2:T(8,128)(2,1)} copy(bf16[64,84,148]{0,2,1:T(8,128)(2,1)} %convert_element_type.78) | data formatting | bytes 3182592 | tf_op jit(solution)/shard_map/convert_element_type | solution.py:134
  131.9 2.7 copy.253
  134.7 2.5 copy.251
  137.2 2.5 copy.249
  139.7 2.5 copy.247
  142.2 2.5 copy.245
  144.8 2.5 copy.243
  147.3 2.5 copy.241
  149.8 2.5 copy.237
  152.3 2.5 copy.239
  154.8 2.7 add_bitcast_fusion
  161.4 2.4 collective-permute-start.7
  165.6 3.3 collective-permute-done.7
  170.6 3.0 fusion.244
  173.7 3.0 fusion.246
  176.7 3.1 fusion.248
  179.8 3.0 fusion.250
  182.8 3.0 fusion.252
  185.9 3.1 fusion.254
  188.9 3.1 fusion.256
  192.0 3.0 fusion.258
  195.0 14.3 %fusion.19 = bf16[64,84,148]{1,0,2:T(8,128)(2,1)S(1)} fusion(f32[84,148,64]{0,2,1:T(8,128)} %fusion.244, f32[84,148,64]{0,2,1:T(8,128)} %fusion.246, f32[84,148,64]{0,2,1:T(8,128)} %fusion.248, f32[84,148,64]{0,2,1:T(8,128)} %fusion.250, f32[84,148,64]{0,2,1:T(8,128)} %fusion.252, f32[84,148,64]{0,2,1:T(8,128)} %fusion.254, f32[84,148,64]{0,2,1:T(8,128)} %fusion.258, ...), kind=kOutput, calls=%fused_computation.21 | convolution fusion | flops 31030272 | bytes 30106624 | tf_op jit(solution)/shard_map/ohw,co->chw/dot_general | solution.py:41
  209.3 3.9 copy.190
  213.2 5.7 %reshape.311 = bf16[64,42,2,74,2]{0,4,3,2,1:T(2,128)(2,1)} reshape(bf16[64,84,148]{0,2,1:T(8,128)(2,1)} %copy.190) | data formatting | bytes 3182592 | tf_op jit(solution)/shard_map/reshape | solution.py:89
  218.9 11.8 %copy.191 = bf16[64,2,2,42,74]{4,2,1,0,3:T(2,128)(2,1)S(1)} copy(bf16[64,2,2,42,74]{0,2,4,1,3:T(2,128)(2,1)} %bitcast.648) | data formatting | bytes 3182592 | tf_op jit(solution)/shard_map/transpose | solution.py:90
  239.0 2.2 fusion.157
  241.2 2.2 copy.201
  243.5 5.0 copy.202
  248.5 2.2 fusion.117
  286.5 80.9 %all-reduce.9.cloned.1.call-done = (f32[3,3,64,64]{3,2,1,0:T(8,128)}, f32[3,3,64,256]{3,2,1,0:T(8,128)}, f32[3,3,64,256]{3,2,1,0:T(8,128)}) async-done(((f32[3,3,64,64]{3,2,1,0:T(8,128)}, f32[3,3,64,256]{3,2,1,0:T(8,128)}, f32[3,3,64,256]{3,2,1,0:T(8,128)}), (f32[3,3,64,64]{3,2,1,0:T(8,128)}, f32[3,3,64,256]{3,2,1,0:T(8,128)}, f32[3,3,64,256]{3,2,1,0:T(8,128)})) %all-reduce.9.cloned.1.call-update) | async-done | bytes 1327120 | tf_op jit(solution)/shard_map/psum | solution.py:154
  368.3 34.1 %all-reduce.2 = (f32[3,3,12,64]{3,2,1,0:T(8,128)S(1)}, f32[3,3,64,12]{2,3,1,0:T(8,128)S(1)}, f32[64]{0:T(128)S(1)}, f32[64]{0:T(128)S(1)}, f32[256]{0:T(256)S(1)}, /*index=5*/f32[256]{0:T(256)S(1)}, f32[12]{0:T(128)S(1)}) all-reduce(f32[3,3,12,64]{3,2,1,0:T(8,128)S(1)} %bitcast.657, ...), channel_id=1, replica_groups=mesh['gx'=8,'gy'=16] {'gx'}, use_global_device_ids=true, to_apply=%region_0.1 | all-reduce | flops 14476 | bytes 115808 | tf_op jit(solution)/shard_map/psum | solution.py:154
  402.5 63.3 %all-reduce = (f32[3,3,12,64]{3,2,1,0:T(8,128)S(1)}, f32[3,3,64,12]{2,3,1,0:T(8,128)S(1)}, f32[64]{0:T(128)S(1)}, f32[64]{0:T(128)S(1)}, f32[256]{0:T(256)S(1)}, /*index=5*/f32[256]{0:T(256)S(1)}, f32[12]{0:T(128)S(1)}) all-reduce(f32[3,3,12,64]{3,2,1,0:T(8,128)S(1)} %get-tuple-element.65, ...), channel_id=1, replica_groups=mesh['gx'=8,'gy'=16] {'gy'}, use_global_device_ids=true, to_apply=%region_1.2 | all-reduce | flops 14476 | bytes 115808 | tf_op jit(solution)/shard_map/psum | solution.py:153
  468.6 26.6 %all-reduce.7.cloned.1.call-done = (f32[3,3,64,64]{3,2,1,0:T(8,128)}, f32[3,3,64,256]{3,2,1,0:T(8,128)}, f32[3,3,64,256]{3,2,1,0:T(8,128)}) async-done(((f32[3,3,64,64]{3,2,1,0:T(8,128)}, f32[3,3,64,256]{3,2,1,0:T(8,128)}, f32[3,3,64,256]{3,2,1,0:T(8,128)}), (f32[3,3,64,64]{3,2,1,0:T(8,128)}, f32[3,3,64,256]{3,2,1,0:T(8,128)}, f32[3,3,64,256]{3,2,1,0:T(8,128)})) %all-reduce.7.cloned.1.call-update) | async-done | bytes 1327120 | tf_op jit(solution)/shard_map/psum | solution.py:153
  496.9 2.4 broadcast_multiply_fusion
  (287 shorter events, 110.9 us)
Async XLA Ops:
  7.2 36.7 %copy-start.22 = (bf16[12,64,128]{2,1,0:T(8,128)(2,1)S(1)}, bf16[12,64,128]{2,1,0:T(8,128)(2,1)}, u32[]{:S(2)}) copy-start(bf16[12,64,128]{2,1,0:T(8,128)(2,1)} %param.23) | copy-start | bytes 589828
  8.7 41.7 %copy-start.41 = (bf16[3,3,12,64]{3,2,1,0:T(8,128)(2,1)S(1)}, bf16[3,3,12,64]{3,2,1,0:T(8,128)(2,1)}, u32[]{:S(2)}) copy-start(bf16[3,3,12,64]{3,2,1,0:T(8,128)(2,1)} %param.13) | copy-start | bytes 41476
  10.9 16.4 %all-to-all-start = ((bf16[16,2,192]{2,1,0:T(2,128)(2,1)}), bf16[16,2,192]{2,1,0:T(2,128)(2,1)S(1)}, u32[]{:S(2)}, u32[]{:S(2)}) async-start(bf16[16,2,192]{2,1,0:T(2,128)(2,1)} %reshape.410), calls=%async_computation | async-start | bytes 32768 | tf_op jit(solution)/shard_map/all_to_all | solution.py:125
  17.3 350.1 %all-reduce.9.cloned.1.call-start = ((), (), s32[]{:S(2)}) async-start(), calls=%async_computation.2 | async-start | bytes 2949120 | tf_op jit(solution)/shard_map/psum | solution.py:154
  19.4 139.1 %collective-permute-start.5 = (bf16[12,11,128]{1,0,2:T(8,128)(2,1)}, bf16[12,11,128]{1,0,2:T(8,128)(2,1)}, u32[]{:S(2)}, u32[]{:S(2)}) collective-permute-start(bf16[12,11,128]{1,0,2:T(8,128)(2,1)} %copy.188), channel_id=1, source_target_pairs={{16,0},{32,16},{48,32},{64,48},{80,64},{96,80},{112,96},{17,1},{33... | collective-permute-start | bytes 101384 | tf_op jit(solution)/shard_map/ppermute | solution.py:15
  21.9 136.5 %collective-permute-start.4 = (bf16[12,11,128]{1,0,2:T(8,128)(2,1)}, bf16[12,11,128]{1,0,2:T(8,128)(2,1)}, u32[]{:S(2)}, u32[]{:S(2)}) collective-permute-start(bf16[12,11,128]{1,0,2:T(8,128)(2,1)} %copy.187), channel_id=1, source_target_pairs={{0,16},{16,32},{32,48},{48,64},{64,80},{80,96},{96,112},{1,17},{17... | collective-permute-start | bytes 101384 | tf_op jit(solution)/shard_map/ppermute | solution.py:12
  27.9 24.0 %copy-start.33 = (bf16[12,16,32]{2,0,1:T(8,128)(2,1)}, bf16[12,16,32]{2,0,1:T(8,128)(2,1)S(1)}, u32[]{:S(2)}) copy-start(bf16[12,16,32]{2,0,1:T(8,128)(2,1)S(1)} %copy.169) | copy-start | bytes 36868
  27.9 9.3 %collective-permute-start = (bf16[12,6,32]{2,0,1:T(8,128)(2,1)S(1)}, bf16[12,6,32]{2,0,1:T(8,128)(2,1)S(1)}, u32[]{:S(2)}, u32[]{:S(2)}) collective-permute-start(bf16[12,6,32]{2,0,1:T(8,128)(2,1)S(1)} %get-tuple-element.82), channel_id=1, source_target_pairs={{0,16},{16,32},{32,48},{48,64},{64,80},{80,96},{96,112},{1,17},{17... | collective-permute-start | bytes 13832 | tf_op jit(solution)/shard_map/ppermute | solution.py:12
  30.3 6.9 %collective-permute-start.1 = (bf16[12,6,32]{2,0,1:T(8,128)(2,1)S(1)}, bf16[12,6,32]{2,0,1:T(8,128)(2,1)S(1)}, u32[]{:S(2)}, u32[]{:S(2)}) collective-permute-start(bf16[12,6,32]{2,0,1:T(8,128)(2,1)S(1)} %get-tuple-element.81), channel_id=1, source_target_pairs={{16,0},{32,16},{48,32},{64,48},{80,64},{96,80},{112,96},{17,1},{33... | collective-permute-start | bytes 13832 | tf_op jit(solution)/shard_map/ppermute | solution.py:15
  37.3 4.7 copy-start.44
  37.3 4.6 copy-start.42
  37.3 15.0 %copy-start.7 = (bf16[12,28,32]{2,0,1:T(8,128)(2,1)}, bf16[12,28,32]{2,0,1:T(8,128)(2,1)S(1)}, u32[]{:S(2)}) copy-start(bf16[12,28,32]{2,0,1:T(8,128)(2,1)S(1)} %constant_dynamic-update-slice_fusion) | copy-start | bytes 64516
  37.4 8.3 %collective-permute-start.2 = (bf16[12,28,6]{2,0,1:T(8,128)(2,1)S(1)}, bf16[12,28,6]{2,0,1:T(8,128)(2,1)S(1)}, u32[]{:S(2)}, u32[]{:S(2)}) collective-permute-start(bf16[12,28,6]{2,0,1:T(8,128)(2,1)S(1)} %get-tuple-element.79), channel_id=1, source_target_pairs={{0,1},{1,2},{2,3},{3,4},{4,5},{5,6},{6,7},{7,8},{8,9},{9,10},{10,1... | collective-permute-start | bytes 12104 | tf_op jit(solution)/shard_map/ppermute | solution.py:12
  41.9 8.2 %collective-permute-start.3 = (bf16[12,28,6]{2,0,1:T(8,128)(2,1)S(1)}, bf16[12,28,6]{2,0,1:T(8,128)(2,1)S(1)}, u32[]{:S(2)}, u32[]{:S(2)}) collective-permute-start(bf16[12,28,6]{2,0,1:T(8,128)(2,1)S(1)} %get-tuple-element.80), channel_id=1, source_target_pairs={{1,0},{2,1},{3,2},{4,3},{5,4},{6,5},{7,6},{8,7},{9,8},{10,9},{11,1... | collective-permute-start | bytes 12104 | tf_op jit(solution)/shard_map/ppermute | solution.py:15
  45.8 6.9 %copy-start.19 = (bf16[12,28,6]{2,0,1:T(8,128)(2,1)}, bf16[12,28,6]{2,0,1:T(8,128)(2,1)S(1)}, u32[]{:S(2)}) copy-start(bf16[12,28,6]{2,0,1:T(8,128)(2,1)S(1)} %collective-permute-done.2) | copy-start | bytes 12100
  50.2 2.5 copy-start.16
  51.2 2.3 copy-start.49
  54.4 2.2 copy-start.5
  56.9 2.3 copy-start.3
  76.4 2.5 copy-start.47
  108.1 1.9 copy-start.36
  122.0 3.4 copy-start.14
  147.3 7.6 %copy-start.51 = (f32[12]{0:T(128)S(1)}, f32[12]{0:T(128)}, u32[]{:S(2)}) copy-start(f32[12]{0:T(128)} %param.22) | copy-start | bytes 148
  154.8 2.7 copy-start.15
  159.5 6.1 %collective-permute-start.6 = (bf16[12,86,11]{1,0,2:T(8,128)(2,1)S(1)}, bf16[12,86,11]{1,0,2:T(8,128)(2,1)S(1)}, u32[]{:S(2)}, u32[]{:S(2)}) collective-permute-start(bf16[12,86,11]{1,0,2:T(8,128)(2,1)S(1)} %get-tuple-element.75), channel_id=1, source_target_pairs={{0,1},{1,2},{2,3},{3,4},{4,5},{5,6},{6,7},{7,8},{8,9},{9,10},{10,1... | collective-permute-start | bytes 68120 | tf_op jit(solution)/shard_map/ppermute | solution.py:12
  161.4 7.5 %collective-permute-start.7 = (bf16[12,86,11]{1,0,2:T(8,128)(2,1)S(1)}, bf16[12,86,11]{1,0,2:T(8,128)(2,1)S(1)}, u32[]{:S(2)}, u32[]{:S(2)}) collective-permute-start(bf16[12,86,11]{1,0,2:T(8,128)(2,1)S(1)} %get-tuple-element.76), channel_id=1, source_target_pairs={{1,0},{2,1},{3,2},{4,3},{5,4},{6,5},{7,6},{8,7},{9,8},{10,9},{11,1... | collective-permute-start | bytes 68120 | tf_op jit(solution)/shard_map/ppermute | solution.py:15
  164.7 9.0 %copy-start.39 = (f32[9,64,12]{1,2,0:T(8,128)}, f32[9,64,12]{1,2,0:T(8,128)S(1)}, u32[]{:S(2)}) copy-start(f32[9,64,12]{1,2,0:T(8,128)S(1)} %fusion.220) | copy-start | bytes 82948
  192.0 3.0 copy-start.2
  248.5 4.3 copy-start
  248.5 4.3 copy-start.26
  257.4 13.2 %copy-start.10 = (bf16[64,18,34]{0,2,1:T(8,128)(2,1)}, bf16[64,18,34]{0,2,1:T(8,128)(2,1)S(1)}, u32[]{:S(2)}) copy-start(bf16[64,18,34]{0,2,1:T(8,128)(2,1)S(1)} %fusion.127) | copy-start | bytes 235012
  269.1 8.5 %copy-start.12 = (bf16[64,16,32]{0,2,1:T(8,128)(2,1)}, bf16[64,16,32]{0,2,1:T(8,128)(2,1)S(1)}, u32[]{:S(2)}) copy-start(bf16[64,16,32]{0,2,1:T(8,128)(2,1)S(1)} %get-tuple-element.84) | copy-start | bytes 196612
  270.8 1.9 copy-start.32
  274.6 2.2 copy-start.8
  274.6 2.2 copy-start.20
  274.6 2.5 copy-start.34
  274.6 2.5 copy-start.45
  274.6 2.7 copy-start.17
  276.7 218.5 %all-reduce.7.cloned.1.call-start = ((), (), s32[]{:S(2)}) async-start(), calls=%async_computation.1 | async-start | bytes 2949120 | tf_op jit(solution)/shard_map/psum | solution.py:153
  277.9 2.0 copy-start.37
  279.9 2.3 copy-start.13
  279.9 3.1 copy-start.9
  279.9 3.1 copy-start.18
  279.9 4.0 copy-start.21
  279.9 4.9 copy-start.35
  279.9 4.9 copy-start.43
  281.9 85.5 %copy-start.11 = (bf16[64,18,34]{0,2,1:T(8,128)(2,1)S(1)}, bf16[64,18,34]{0,2,1:T(8,128)(2,1)}, u32[]{:S(2)}) copy-start(bf16[64,18,34]{0,2,1:T(8,128)(2,1)} %copy-done.10) | copy-start | bytes 235012
  281.9 85.6 %copy-start.1 = (bf16[64,2,2,20,36]{4,2,1,0,3:T(2,128)(2,1)S(1)}, bf16[64,2,2,20,36]{4,2,1,0,3:T(2,128)(2,1)}, u32[]{:S(2)}) copy-start(bf16[64,2,2,20,36]{4,2,1,0,3:T(2,128)(2,1)} %copy.202) | copy-start | bytes 1105924
  (15 other events, 17.9 us)
Sparse Core Ops, SparseCore 0:
  276.8 90.5 all-reduce.8
  370.1 125.0 all-reduce.6
